TPU v7x, 128 devices: a whole 4x4x4 slice. The times are simulated.
128 devices in a mesh: shard: 64 (over z, y, x_hi, core), tensor: 2 (over x_lo).
Axes of the slice: x: 4 (x_hi: 2, x_lo: 2; x = x_hi * 2 + x_lo), y: 4, z: 4, core: 2. Of those that a mesh axis runs over, the one named last changes fastest.
Arguments:
- grads: float32 [64, 2048, 1024], P(None, 'shard', 'tensor'), may hold values from -16 to 16
- momentum: bfloat16 [64, 2048, 1024], P(None, 'shard', 'tensor'), may hold values from -32 to 32
- counts: int32 [1], replicated, may hold values from 1 to 8
- emb_grad: float32 [8192, 2048], P('shard', 'tensor'), may hold values from -6 to 6
- emb_weight: float32 [8192, 2048], P('shard', 'tensor'), may hold values from -6 to 6
- emb_first: float32 [8192, 2048], P('shard', 'tensor'), may hold values from -2 to 2
- emb_second: float32 [8192, 2048], P('shard', 'tensor'), may hold values from 0.01 to 1
- gain_grad: float32 [65536], P(('shard', 'tensor')), may hold values from -6 to 6
- gain_weight: float32 [65536], P(('shard', 'tensor')), may hold values from 0.5 to 1.5
- gain_first: float32 [65536], P(('shard', 'tensor')), may hold values from -2 to 2
- gain_second: float32 [65536], P(('shard', 'tensor')), may hold values from 0.01 to 1
Outputs:
- new_momentum: bfloat16 [64, 2048, 1024], P(None, 'shard', 'tensor')
- update: float32 [64, 2048, 1024], P(None, 'shard', 'tensor')
- emb_weight_new: float32 [8192, 2048], P('shard', 'tensor')
- emb_first_new: float32 [8192, 2048], P('shard', 'tensor')
- emb_second_new: float32 [8192, 2048], P('shard', 'tensor')
- gain_weight_new: float32 [65536], P(('shard', 'tensor'))
- gain_first_new: float32 [65536], P(('shard', 'tensor'))
- gain_second_new: float32 [65536], P(('shard', 'tensor'))
All inputs are finite; a program needn't handle non-finite values.
Results may differ from a plain program's by a relative error of at most 0.012.
The roundings to bfloat16 on the way count: a program that leaves them out, or rounds other values in their place, can miss the bound.
Values may be sent and summed in bfloat16 or wider, within the bound.
A program may use at most 128 MiB of HBM per device.

v0:
```python
import math

import jax
import jax.numpy as jnp
from jax import lax
from jax.sharding import PartitionSpec as P

D = 2048
NS_STEPS = 4


linear_coef = 3.4445
cubic_coef = -4.775
quintic_coef = 2.0315
momentum_rate = 0.95
learn_rate = 0.01
decay_weight = 0.1
first_rate = 0.9
second_rate = 0.95
adam_floor = 1e-08
norm_floor = 1e-07


def adamw(grad, weight, first, second, inverse):
    scaled = grad * inverse
    first_new = first_rate * first + (1.0 - first_rate) * scaled
    second_new = second_rate * second + (1.0 - second_rate) * scaled * scaled
    weight_new = weight - learn_rate * (
        first_new / (jnp.sqrt(second_new) + adam_floor) + decay_weight * weight
    )
    return (weight_new, first_new, second_new)


def combine(iterate, product, quintic, final):
    mixed = (
        linear_coef * iterate.astype(jnp.float32) + cubic_coef * product + quintic_coef * quintic
    )
    if final:
        return mixed * math.sqrt(D)
    return mixed.astype(jnp.bfloat16)


def columns_layout(iterate):
    for number in range(NS_STEPS):
        whole = lax.all_gather(iterate, "tensor", axis=1, tiled=True)
        gram = jnp.einsum("ri,rc->ic", whole, iterate, preferred_element_type=jnp.float32).astype(
            jnp.bfloat16
        )
        product = jnp.dot(whole, gram, preferred_element_type=jnp.float32)
        product_whole = lax.all_gather(product.astype(jnp.bfloat16), "tensor", axis=1, tiled=True)
        quintic = jnp.dot(product_whole, gram, preferred_element_type=jnp.float32)
        iterate = combine(iterate, product, quintic, number + 1 == NS_STEPS)
    return iterate


def body(
    grads,
    momentum,
    counts,
    emb_grad,
    emb_weight,
    emb_first,
    emb_second,
    gain_grad,
    gain_weight,
    gain_first,
    gain_second,
):
    inverse = 1.0 / counts[0].astype(jnp.float32)
    scaled = grads * inverse
    velocity = momentum_rate * momentum.astype(jnp.float32) + scaled
    advance = scaled + momentum_rate * velocity
    owned = lax.all_to_all(advance, "shard", split_axis=0, concat_axis=1, tiled=True)[0]
    total = jnp.sqrt(lax.psum(jnp.sum(owned * owned), "tensor"))
    iterate = (owned / (total + norm_floor)).astype(jnp.bfloat16)
    finished = columns_layout(iterate)
    blocks = finished.reshape(lax.axis_size("shard"), -1, finished.shape[1])
    update = lax.all_to_all(
        blocks.astype(jnp.bfloat16), "shard", split_axis=0, concat_axis=0, tiled=True
    ).astype(blocks.dtype)
    emb_new = adamw(emb_grad, emb_weight, emb_first, emb_second, inverse)
    gain_new = adamw(gain_grad, gain_weight, gain_first, gain_second, inverse)
    return (
        velocity.astype(jnp.bfloat16),
        update,
        emb_new[0],
        emb_new[1],
        emb_new[2],
        gain_new[0],
        gain_new[1],
        gain_new[2],
    )


def solution(mesh):
    placed = (
        P(None, "shard", "tensor"),
        P(None, "shard", "tensor"),
        P(),
        P("shard", "tensor"),
        P("shard", "tensor"),
        P("shard", "tensor"),
        P("shard", "tensor"),
        P(("shard", "tensor")),
        P(("shard", "tensor")),
        P(("shard", "tensor")),
        P(("shard", "tensor")),
    )
    return jax.shard_map(
        body,
        mesh=mesh,
        in_specs=placed,
        out_specs=(
            P(None, "shard", "tensor"),
            P(None, "shard", "tensor"),
            P("shard", "tensor"),
            P("shard", "tensor"),
            P("shard", "tensor"),
            P(("shard", "tensor")),
            P(("shard", "tensor")),
            P(("shard", "tensor")),
        ),
        check_vma=False,
    )
```

profile of v0, /device:TPU:1, one launch (start us, length us, event | category | flops | bytes accessed | tf_op | source)
XLA Modules:
  0.0 695.3 jit_solution(10698795996843532330)
XLA Ops:
  7.2 0.0 all-gather.9.cloned.1.call-start
  7.9 5.2 multiply_add_fusion
  13.1 65.8 %all_to_all.14 = f32[64,32,512]{2,1,0:T(8,128)S(1)} all-to-all(f32[64,32,512]{2,1,0:T(8,128)S(1)} %get-tuple-element.14), channel_id=1, replica_groups=mesh['shard'=64,'tensor'=2] {'shard'}, dimensions={0} | all-to-all | bytes 8388608 | tf_op jit(solution)/shard_map/all_to_all | solution.py:73
  78.9 2.0 copy-done
  80.9 1.7 multiply_reduce_fusion
  82.6 4.4 psum.7
  87.6 4.2 divide_convert_fusion
  91.8 0.0 all-gather.9.cloned.1.call-update
  91.9 0.0 all-gather.11.cloned.1.call-start
  91.9 56.0 %all-gather.9.cloned.1.call-done = bf16[2048,1024]{1,0:T(8,128)(2,1)} async-done(((bf16[2048,512]{1,0:T(8,128)(2,1)}), bf16[2048,1024]{1,0:T(8,128)(2,1)}) %all-gather.9.cloned.1.call-update) | async-done | bytes 4194320 | tf_op jit(solution)/shard_map/all_gather | solution.py:45
  147.9 5.4 convolution_convert_fusion.3
  153.2 0.0 copy-done.11
  153.2 0.0 copy-start.1
  153.2 5.3 fusion.5
  158.5 0.0 all-gather.11.cloned.1.call-update
  158.5 0.0 all-gather.13.cloned.1.call-start
  158.6 60.3 %all-gather.11.cloned.1.call-done = bf16[2048,1024]{1,0:T(8,128)(2,1)} async-done(((bf16[2048,512]{1,0:T(8,128)(2,1)}), bf16[2048,1024]{1,0:T(8,128)(2,1)}) %all-gather.11.cloned.1.call-update) | async-done | bytes 4194320 | tf_op jit(solution)/shard_map/all_gather | solution.py:50
  218.9 0.0 copy-done.1
  218.9 7.7 %add_convert_fusion.2 = bf16[2048,512]{1,0:T(8,128)(2,1)} fusion(f32[2048,512]{1,0:T(8,128)} %get-tuple-element.17, bf16[2048,512]{1,0:T(8,128)(2,1)S(1)} %bitcast.29, bf16[2048,1024]{1,0:T(8,128)(2,1)} %all-gather.11.cloned.1.call-done, bf16[1024,512]{1,0:T(8,128)(2,1)S(1)} %convolution_convert_fusion.3), kind=kOutput, calls=%fused_computation.3 | convolution fusion | flops 2154823680 | bytes 13631488 | tf_op jit(solution)/shard_map/dot_general | solution.py:51
  226.6 0.0 all-gather.13.cloned.1.call-update
  226.6 0.2 all-gather.15.cloned.1.call-start
  226.9 60.1 %all-gather.13.cloned.1.call-done = bf16[2048,1024]{1,0:T(8,128)(2,1)} async-done(((bf16[2048,512]{1,0:T(8,128)(2,1)}), bf16[2048,1024]{1,0:T(8,128)(2,1)}) %all-gather.13.cloned.1.call-update) | async-done | bytes 4194320 | tf_op jit(solution)/shard_map/all_gather | solution.py:45
  287.0 5.4 convolution_convert_fusion.2
  292.4 0.0 copy-done.12
  292.4 0.0 copy-start.2
  292.4 5.3 fusion.6
  297.7 0.0 all-gather.15.cloned.1.call-update
  297.7 0.0 all-gather.17.cloned.1.call-start
  297.7 60.3 %all-gather.15.cloned.1.call-done = bf16[2048,1024]{1,0:T(8,128)(2,1)} async-done(((bf16[2048,512]{1,0:T(8,128)(2,1)}), bf16[2048,1024]{1,0:T(8,128)(2,1)}) %all-gather.15.cloned.1.call-update) | async-done | bytes 4194320 | tf_op jit(solution)/shard_map/all_gather | solution.py:50
  358.0 0.0 copy-done.2
  358.0 7.7 %add_convert_fusion.1 = bf16[2048,512]{1,0:T(8,128)(2,1)} fusion(f32[2048,512]{1,0:T(8,128)} %get-tuple-element.19, bf16[2048,512]{1,0:T(8,128)(2,1)S(1)} %copy-done.2, bf16[2048,1024]{1,0:T(8,128)(2,1)} %all-gather.15.cloned.1.call-done, bf16[1024,512]{1,0:T(8,128)(2,1)S(1)} %convolution_convert_fusion.2), kind=kOutput, calls=%fused_computation.2 | convolution fusion | flops 2154823680 | bytes 13631488 | tf_op jit(solution)/shard_map/dot_general | solution.py:51
  365.8 0.0 all-gather.17.cloned.1.call-update
  365.8 0.0 all-gather.19.cloned.1.call-start
  365.8 60.3 %all-gather.17.cloned.1.call-done = bf16[2048,1024]{1,0:T(8,128)(2,1)} async-done(((bf16[2048,512]{1,0:T(8,128)(2,1)}), bf16[2048,1024]{1,0:T(8,128)(2,1)}) %all-gather.17.cloned.1.call-update) | async-done | bytes 4194320 | tf_op jit(solution)/shard_map/all_gather | solution.py:45
  426.1 5.4 convolution_convert_fusion.1
  431.5 0.0 copy-done.13
  431.5 0.0 copy-start.3
  431.5 5.3 fusion.7
  436.8 0.0 all-gather.19.cloned.1.call-update
  436.8 0.3 all-gather.21.cloned.1.call-start
  437.1 60.1 %all-gather.19.cloned.1.call-done = bf16[2048,1024]{1,0:T(8,128)(2,1)} async-done(((bf16[2048,512]{1,0:T(8,128)(2,1)}), bf16[2048,1024]{1,0:T(8,128)(2,1)}) %all-gather.19.cloned.1.call-update) | async-done | bytes 4194320 | tf_op jit(solution)/shard_map/all_gather | solution.py:50
  497.2 0.0 copy-done.3
  497.2 7.7 %add_convert_fusion = bf16[2048,512]{1,0:T(8,128)(2,1)} fusion(f32[2048,512]{1,0:T(8,128)} %get-tuple-element.21, bf16[2048,512]{1,0:T(8,128)(2,1)S(1)} %copy-done.3, bf16[2048,1024]{1,0:T(8,128)(2,1)} %all-gather.19.cloned.1.call-done, bf16[1024,512]{1,0:T(8,128)(2,1)S(1)} %convolution_convert_fusion.1), kind=kOutput, calls=%fused_computation.1 | convolution fusion | flops 2154823680 | bytes 13631488 | tf_op jit(solution)/shard_map/dot_general | solution.py:51
  504.9 0.0 all-gather.21.cloned.1.call-update
  504.9 0.0 all-gather.23.cloned.1.call-start
  505.0 60.3 %all-gather.21.cloned.1.call-done = bf16[2048,1024]{1,0:T(8,128)(2,1)} async-done(((bf16[2048,512]{1,0:T(8,128)(2,1)}), bf16[2048,1024]{1,0:T(8,128)(2,1)}) %all-gather.21.cloned.1.call-update) | async-done | bytes 4194320 | tf_op jit(solution)/shard_map/all_gather | solution.py:45
  565.3 5.4 convolution_convert_fusion
  570.6 0.0 copy-done.14
  570.6 0.0 copy-start.4
  570.7 5.3 fusion.8
  575.9 0.0 all-gather.23.cloned.1.call-update
  576.0 60.3 %all-gather.23.cloned.1.call-done = bf16[2048,1024]{1,0:T(8,128)(2,1)} async-done(((bf16[2048,512]{1,0:T(8,128)(2,1)}), bf16[2048,1024]{1,0:T(8,128)(2,1)}) %all-gather.23.cloned.1.call-update) | async-done | bytes 4194320 | tf_op jit(solution)/shard_map/all_gather | solution.py:50
  636.3 7.9 %multiply_convert_fusion = bf16[2048,512]{1,0:T(8,128)(2,1)} fusion(f32[2048,512]{1,0:T(8,128)} %get-tuple-element.23, bf16[2048,512]{1,0:T(8,128)(2,1)S(1)} %copy-done.4, bf16[2048,1024]{1,0:T(8,128)(2,1)} %all-gather.23.cloned.1.call-done, bf16[1024,512]{1,0:T(8,128)(2,1)S(1)} %convolution_convert_fusion), kind=kOutput, calls=%fused_computation | convolution fusion | flops 2155872256 | bytes 13631488 | tf_op jit(solution)/shard_map/dot_general | solution.py:51
  644.2 0.0 copy-start.5
  644.2 0.0 copy-start.6
  644.2 10.5 %all-to-all-start.1 = ((bf16[64,32,512]{2,1,0:T(8,128)(2,1)}), bf16[64,32,512]{2,1,0:T(8,128)(2,1)S(1)}, u32[]{:S(2)}, u32[]{:S(2)}) async-start(bf16[64,32,512]{2,1,0:T(8,128)(2,1)} %bitcast.30), calls=%async_computation.1 | async-start | bytes 4194304 | tf_op jit(solution)/shard_map/all_to_all | solution.py:78
  654.8 0.0 copy-done.7
  654.8 0.0 copy-done.8
  654.8 0.0 copy-done.9
  654.8 0.0 copy-done.10
  654.8 0.6 multiply_subtract_fusion.1
  655.4 2.6 multiply_subtract_fusion
  658.0 27.8 %all-to-all-done.1 = bf16[64,32,512]{2,1,0:T(8,128)(2,1)S(1)} async-done(((bf16[64,32,512]{2,1,0:T(8,128)(2,1)}), bf16[64,32,512]{2,1,0:T(8,128)(2,1)S(1)}, u32[]{:S(2)}, u32[]{:S(2)}) %all-to-all-start.1) | async-done | bytes 2097184 | tf_op jit(solution)/shard_map/all_to_all | solution.py:78
  685.8 2.6 convert_element_type.92
  (12 shorter events, 0.0 us)
Async XLA Ops:
  7.2 140.7 %all-gather.9.cloned.1.call-start = ((), (), s32[]{:S(2)}) async-start(), calls=%async_computation.2 | async-start | bytes 6291456 | tf_op jit(solution)/shard_map/all_gather | solution.py:45
  78.9 2.0 copy-start
  91.9 127.1 %all-gather.11.cloned.1.call-start = ((), (), s32[]{:S(2)}) async-start(), calls=%async_computation.3 | async-start | bytes 6291456 | tf_op jit(solution)/shard_map/all_gather | solution.py:50
  147.9 5.4 copy-start.11
  153.2 65.7 %copy-start.1 = (bf16[64,32,512]{2,1,0:T(8,128)(2,1)S(1)}, bf16[64,32,512]{2,1,0:T(8,128)(2,1)}, u32[]{:S(2)}) copy-start(bf16[64,32,512]{2,1,0:T(8,128)(2,1)} %divide_convert_fusion) | copy-start | bytes 6291460
  158.5 128.5 %all-gather.13.cloned.1.call-start = ((), (), s32[]{:S(2)}) async-start(), calls=%async_computation.4 | async-start | bytes 6291456 | tf_op jit(solution)/shard_map/all_gather | solution.py:45
  226.6 131.4 %all-gather.15.cloned.1.call-start = ((), (), s32[]{:S(2)}) async-start(), calls=%async_computation.5 | async-start | bytes 6291456 | tf_op jit(solution)/shard_map/all_gather | solution.py:50
  287.0 5.4 copy-start.12
  292.4 65.7 %copy-start.2 = (bf16[2048,512]{1,0:T(8,128)(2,1)S(1)}, bf16[2048,512]{1,0:T(8,128)(2,1)}, u32[]{:S(2)}) copy-start(bf16[2048,512]{1,0:T(8,128)(2,1)} %add_convert_fusion.2) | copy-start | bytes 6291460
  297.7 128.4 %all-gather.17.cloned.1.call-start = ((), (), s32[]{:S(2)}) async-start(), calls=%async_computation.6 | async-start | bytes 6291456 | tf_op jit(solution)/shard_map/all_gather | solution.py:45
  365.8 131.4 %all-gather.19.cloned.1.call-start = ((), (), s32[]{:S(2)}) async-start(), calls=%async_computation.7 | async-start | bytes 6291456 | tf_op jit(solution)/shard_map/all_gather | solution.py:50
  426.1 5.4 copy-start.13
  431.5 65.7 %copy-start.3 = (bf16[2048,512]{1,0:T(8,128)(2,1)S(1)}, bf16[2048,512]{1,0:T(8,128)(2,1)}, u32[]{:S(2)}) copy-start(bf16[2048,512]{1,0:T(8,128)(2,1)} %add_convert_fusion.1) | copy-start | bytes 6291460
  436.8 128.4 %all-gather.21.cloned.1.call-start = ((), (), s32[]{:S(2)}) async-start(), calls=%async_computation.8 | async-start | bytes 6291456 | tf_op jit(solution)/shard_map/all_gather | solution.py:45
  504.9 131.4 %all-gather.23.cloned.1.call-start = ((), (), s32[]{:S(2)}) async-start(), calls=%async_computation.9 | async-start | bytes 6291456 | tf_op jit(solution)/shard_map/all_gather | solution.py:50
  565.3 5.4 copy-start.14
  570.6 65.7 %copy-start.4 = (bf16[2048,512]{1,0:T(8,128)(2,1)S(1)}, bf16[2048,512]{1,0:T(8,128)(2,1)}, u32[]{:S(2)}) copy-start(bf16[2048,512]{1,0:T(8,128)(2,1)} %add_convert_fusion) | copy-start | bytes 6291460
  644.2 10.6 %copy-start.7 = (f32[512]{0:T(512)S(1)}, f32[512]{0:T(512)}, u32[]{:S(2)}) copy-start(f32[512]{0:T(512)} %param.19) | copy-start | bytes 6148
  644.2 10.6 %copy-start.8 = (f32[512]{0:T(512)S(1)}, f32[512]{0:T(512)}, u32[]{:S(2)}) copy-start(f32[512]{0:T(512)} %param.18) | copy-start | bytes 6148
  644.2 10.6 %copy-start.9 = (f32[512]{0:T(512)S(1)}, f32[512]{0:T(512)}, u32[]{:S(2)}) copy-start(f32[512]{0:T(512)} %param.21) | copy-start | bytes 6148
  644.2 10.6 %copy-start.10 = (f32[512]{0:T(512)S(1)}, f32[512]{0:T(512)}, u32[]{:S(2)}) copy-start(f32[512]{0:T(512)} %param.20) | copy-start | bytes 6148
  644.2 11.2 %copy-start.5 = (f32[128,1024]{1,0:T(8,128)S(1)}, f32[128,1024]{1,0:T(8,128)}, u32[]{:S(2)}) copy-start(f32[128,1024]{1,0:T(8,128)} %param.15) | copy-start | bytes 1572868
  644.2 11.2 %copy-start.6 = (f32[128,1024]{1,0:T(8,128)S(1)}, f32[128,1024]{1,0:T(8,128)}, u32[]{:S(2)}) copy-start(f32[128,1024]{1,0:T(8,128)} %param.14) | copy-start | bytes 1572868
  644.2 41.6 %all-to-all-start.1 = ((bf16[64,32,512]{2,1,0:T(8,128)(2,1)}), bf16[64,32,512]{2,1,0:T(8,128)(2,1)S(1)}, u32[]{:S(2)}, u32[]{:S(2)}) async-start(bf16[64,32,512]{2,1,0:T(8,128)(2,1)} %bitcast.30), calls=%async_computation.1 | async-start | bytes 4194304 | tf_op jit(solution)/shard_map/all_to_all | solution.py:78
Sparse Core Ops, SparseCore 0:
  92.0 55.8 all-gather.8
  158.7 60.2 all-gather.10
  226.8 60.1 all-gather.12
  297.8 60.1 all-gather.14
  365.9 60.1 all-gather.16
  436.9 60.1 all-gather.18
  505.0 60.1 all-gather.20
  576.1 60.1 all-gather.22
where the time goes:
time: 696 us; the launch traced here: 695 us
  waiting for transfers between devices  506 us (73%)
  matrix products  73.5 us (11%)
  blocking collectives  70.2 us (10%)
  other arithmetic  16.9 us (2%)
  between operations  15.7 us (2%)
  starting transfers between devices  11.3 us (2%)
    all_gather x4, waiting for transfers between devices, columns_layout(): lax.all_gather(product.astype(jnp.bfloat16), 'tensor', axis=1, tiled=True)  241 us
    all_gather x4, waiting for transfers between devices, columns_layout(): whole = lax.all_gather(iterate, 'tensor', axis=1, tiled=True)  237 us
    all_to_all x1, blocking collectives, body(): lax.all_to_all(advance, 'shard', split_axis=0, concat_axis=1, tiled=True)[0]  65.8 us
    dot_general x4, matrix products, columns_layout(): quintic = jnp.dot(product_whole, gram, preferred_element_type=jnp.float32)  31 us
    all_to_all x1, waiting for transfers between devices, body(): lax.all_to_all(blocks.astype(jnp.bfloat16), 'shard', split_axis=0, concat...  27.8 us
    dot_general x4, matrix products, columns_layout(): jnp.einsum('ri,rc->ic', whole, iterate, preferred_element_type=jnp.float32)  21.4 us
    dot_general x4, matrix products, columns_layout(): product = jnp.dot(whole, gram, preferred_element_type=jnp.float32)  21.1 us
  transfers between devices with their start and end apart: 9, of which 9 were waited for; matrix products, arithmetic and copies ran while one was open for 0% of the time, Pallas kernels for 0%

commit v1 on v0

v1 whole, which is shorter than its diff:
```python
import math

import jax
import jax.numpy as jnp
from jax import lax
from jax.experimental import pallas as pl
from jax.experimental.pallas import tpu as pltpu
from jax.sharding import PartitionSpec as P

D = 2048
NS_STEPS = 4

linear_coef = 3.4445
cubic_coef = -4.775
quintic_coef = 2.0315
momentum_rate = 0.95
learn_rate = 0.01
decay_weight = 0.1
first_rate = 0.9
second_rate = 0.95
adam_floor = 1e-08
norm_floor = 1e-07

MESH = pl.DeviceIdType.MESH
WIDE = 1024
BLOCK = 256
SIDE = WIDE // BLOCK
STARTS = [0, 4, 7, 9]
UPPER = 10


def adamw(grad, weight, first, second, inverse):
    scaled = grad * inverse
    first_new = first_rate * first + (1.0 - first_rate) * scaled
    second_new = second_rate * second + (1.0 - second_rate) * scaled * scaled
    weight_new = weight - learn_rate * (
        first_new / (jnp.sqrt(second_new) + adam_floor) + decay_weight * weight
    )
    return (weight_new, first_new, second_new)


def advance_kernel(counts_ref, grads_ref, momentum_ref, new_ref, out_ref):
    inverse = 1.0 / counts_ref[0].astype(jnp.float32)

    def step(k, carry):
        scaled = grads_ref[k] * inverse
        velocity = momentum_rate * momentum_ref[k].astype(jnp.float32) + scaled
        new_ref[k] = velocity.astype(jnp.bfloat16)
        advance = (scaled + momentum_rate * velocity).astype(jnp.bfloat16)
        out_ref[k // 2, 0, k % 2] = advance[:16]
        out_ref[k // 2, 1, k % 2] = advance[16:]
        return carry

    lax.fori_loop(0, grads_ref.shape[0], step, 0)


def advance(counts, grads, momentum):
    group = 8
    return pl.pallas_call(
        advance_kernel,
        grid=(64 // group,),
        in_specs=[
            pl.BlockSpec(memory_space=pltpu.SMEM),
            pl.BlockSpec((group, 32, 512), lambda i: (i, 0, 0)),
            pl.BlockSpec((group, 32, 512), lambda i: (i, 0, 0)),
        ],
        out_specs=[
            pl.BlockSpec((group, 32, 512), lambda i: (i, 0, 0)),
            pl.BlockSpec((group // 2, 2, 2, 16, 512), lambda i: (i, 0, 0, 0, 0)),
        ],
        out_shape=[
            jax.ShapeDtypeStruct((64, 32, 512), jnp.bfloat16),
            jax.ShapeDtypeStruct((32, 2, 2, 16, 512), jnp.bfloat16),
        ],
    )(counts, grads, momentum)


def place_kernel(in_ref, out_ref):
    def step(k, carry):
        for c in range(2):
            out_ref[k, 16 * c : 16 * c + 16] = in_ref[k // 2, c, k % 2].astype(jnp.float32)
        return carry

    lax.fori_loop(0, out_ref.shape[0], step, 0)


def place(blocks):
    group = 8
    return pl.pallas_call(
        place_kernel,
        grid=(64 // group,),
        in_specs=[pl.BlockSpec((group // 2, 2, 2, 16, 512), lambda i: (i, 0, 0, 0, 0))],
        out_specs=pl.BlockSpec((group, 32, 512), lambda i: (i, 0, 0)),
        out_shape=jax.ShapeDtypeStruct((64, 32, 512), jnp.float32),
    )(blocks)


def orthogonalize_kernel(
    in_ref, out_ref, x, g, p, ours, theirs, total, total_in, send_sem, recv_sem, norm_send, norm_recv
):
    shard, tensor = lax.axis_index("shard"), lax.axis_index("tensor")
    other = (shard + 1 - 2 * (shard % 2), tensor)
    barrier = pltpu.get_barrier_semaphore()
    pl.semaphore_signal(barrier, inc=1, device_id=other, device_id_type=MESH)

    total[...] = jnp.zeros_like(total)

    def take(s, carry):
        rows = pl.ds(pl.multiple_of(s * 16, 16), 16)
        squares = jnp.zeros((8, 128), jnp.float32)
        for t in range(2):
            part = in_ref[s, t]
            x[rows, 512 * t : 512 * t + 512] = part
            wide = part.astype(jnp.float32)
            wide = wide * wide
            for j in range(4):
                cut = wide[:, 128 * j : 128 * j + 128]
                squares = squares + cut[:8] + cut[8:]
        total[...] += squares
        return carry

    lax.fori_loop(0, 64, take, 0)
    pl.semaphore_wait(barrier, 1)

    norm_copy = pltpu.make_async_remote_copy(
        total, total_in, norm_send, norm_recv, device_id=other, device_id_type=MESH
    )
    norm_copy.start()

    def send(slot, i):
        blocks = pl.ds(STARTS[i], SIDE - i)
        return pltpu.make_async_remote_copy(
            ours.at[slot, blocks],
            theirs.at[slot, blocks],
            send_sem.at[slot, i],
            recv_sem.at[slot, i],
            device_id=other,
            device_id_type=MESH,
        )

    def iterate(slot, gram_scale):
        for i in range(SIDE):
            left = x[:, BLOCK * i : BLOCK * i + BLOCK]
            for j in range(i, SIDE):
                block = lax.dot_general(
                    left,
                    x[:, BLOCK * j : BLOCK * j + BLOCK],
                    (((0,), (0,)), ((), ())),
                    preferred_element_type=jnp.float32,
                )
                ours[slot, STARTS[i] + j - i] = block.astype(jnp.bfloat16)
            send(slot, i).start()
        if gram_scale is None:
            norm_copy.wait()
            norm = jnp.sqrt(jnp.sum(total[...] + total_in[...])) + norm_floor
            gram_scale = 1.0 / (norm * norm)
            result_scale = 1.0 / norm
        else:
            result_scale = None
        for j in range(SIDE):
            send(slot, j).wait()
            for k in range(j, SIDE):
                number = STARTS[j] + k - j
                block = ours[slot, number].astype(jnp.float32) + theirs[slot, number].astype(jnp.float32)
                if result_scale is not None:
                    block = block * gram_scale
                g[BLOCK * j : BLOCK * j + BLOCK, BLOCK * k : BLOCK * k + BLOCK] = block.astype(jnp.bfloat16)
                if k > j:
                    g[BLOCK * k : BLOCK * k + BLOCK, BLOCK * j : BLOCK * j + BLOCK] = block.T.astype(
                        jnp.bfloat16
                    )

            def multiply(r, carry):
                rows = pl.ds(pl.multiple_of(r * BLOCK, BLOCK), BLOCK)
                p[rows, BLOCK * j : BLOCK * j + BLOCK] = jnp.dot(
                    x[rows, :], g[:, BLOCK * j : BLOCK * j + BLOCK], preferred_element_type=jnp.float32
                )
                return carry

            lax.fori_loop(0, SIDE, multiply, 0)
        return result_scale

    def combined(rows):
        product = p[rows, :]
        quintic = jnp.dot(product.astype(jnp.bfloat16), g[...], preferred_element_type=jnp.float32)
        return linear_coef * x[rows, :].astype(jnp.float32) + cubic_coef * product + quintic_coef * quintic

    def advance_rows(scale):
        def body(r, carry):
            rows = pl.ds(pl.multiple_of(r * BLOCK, BLOCK), BLOCK)
            mixed = combined(rows)
            if scale is not None:
                mixed = mixed * scale
            x[rows, :] = mixed.astype(jnp.bfloat16)
            return carry

        lax.fori_loop(0, SIDE, body, 0)

    advance_rows(iterate(0, None))

    def middle(n, carry):
        iterate(lax.rem(n, 2), 1.0)
        advance_rows(None)
        return carry

    lax.fori_loop(1, NS_STEPS - 1, middle, 0)

    iterate((NS_STEPS - 1) % 2, 1.0)

    def finish(r, carry):
        rows = pl.ds(pl.multiple_of(r * BLOCK, BLOCK), BLOCK)
        mixed = (combined(rows) * math.sqrt(D)).astype(jnp.bfloat16)
        for s in range(BLOCK // 16):
            for t in range(2):
                out_ref[r * (BLOCK // 16) + s, t] = mixed[16 * s : 16 * s + 16, 512 * t : 512 * t + 512]
        return carry

    lax.fori_loop(0, SIDE, finish, 0)


def orthogonalize(blocks):
    vmem = pl.BlockSpec(memory_space=pltpu.VMEM)
    return pl.pallas_call(
        orthogonalize_kernel,
        out_shape=jax.ShapeDtypeStruct((64, 2, 16, 512), jnp.bfloat16),
        in_specs=[vmem],
        out_specs=vmem,
        scratch_shapes=[
            pltpu.VMEM((WIDE, WIDE), jnp.bfloat16),
            pltpu.VMEM((WIDE, WIDE), jnp.bfloat16),
            pltpu.VMEM((WIDE, WIDE), jnp.float32),
            pltpu.VMEM((2, UPPER, BLOCK, BLOCK), jnp.bfloat16),
            pltpu.VMEM((2, UPPER, BLOCK, BLOCK), jnp.bfloat16),
            pltpu.VMEM((8, 128), jnp.float32),
            pltpu.VMEM((8, 128), jnp.float32),
            pltpu.SemaphoreType.DMA((2, SIDE)),
            pltpu.SemaphoreType.DMA((2, SIDE)),
            pltpu.SemaphoreType.DMA,
            pltpu.SemaphoreType.DMA,
        ],
        compiler_params=pltpu.CompilerParams(
            collective_id=1, has_side_effects=True, vmem_limit_bytes=40 * 2**20
        ),
    )(blocks)


def body(
    grads,
    momentum,
    counts,
    emb_grad,
    emb_weight,
    emb_first,
    emb_second,
    gain_grad,
    gain_weight,
    gain_first,
    gain_second,
):
    inverse = 1.0 / counts[0].astype(jnp.float32)
    new_momentum, blocks = advance(counts, grads, momentum)
    owned = lax.all_to_all(
        blocks.reshape(128, 16, 512), ("shard", "tensor"), split_axis=0, concat_axis=0, tiled=True
    )
    finished = orthogonalize(owned.reshape(64, 2, 16, 512))
    back = lax.all_to_all(
        finished.reshape(128, 16, 512), ("shard", "tensor"), split_axis=0, concat_axis=0, tiled=True
    )
    update = place(back.reshape(32, 2, 2, 16, 512))
    emb_new = adamw(emb_grad, emb_weight, emb_first, emb_second, inverse)
    gain_new = adamw(gain_grad, gain_weight, gain_first, gain_second, inverse)
    return (
        new_momentum,
        update,
        emb_new[0],
        emb_new[1],
        emb_new[2],
        gain_new[0],
        gain_new[1],
        gain_new[2],
    )


def solution(mesh):
    matrix = P(None, "shard", "tensor")
    table = P("shard", "tensor")
    gains = P(("shard", "tensor"))
    return jax.shard_map(
        body,
        mesh=mesh,
        in_specs=(matrix, matrix, P(), table, table, table, table, gains, gains, gains, gains),
        out_specs=(matrix, matrix, table, table, table, gains, gains, gains),
        check_vma=False,
    )
```

time: 696 us -> 141 us (0.20)
  waiting for transfers between devices: 506 us -> 27.2 us
  matrix products: 73.5 us -> 0 us
  Pallas kernels: 0 us -> 61.3 us
  blocking collectives: 70.2 us -> 41.9 us
  between operations: 15.7 us -> 1.42 us
  other arithmetic: 16.9 us -> 3.19 us
  starting transfers between devices: 11.3 us -> 3.87 us
    all_gather x8 -> x0, waiting for transfers between devices: 478 us -> none  [the longest x4 241 us: columns_layout(): lax.all_gather(product.astype(jnp.bfloat16), 'tensor', axis=1, tiled=True)]
    dot_general x12 -> x0, matrix products: 73.5 us -> none  [the longest x4 31 us: columns_layout(): quintic = jnp.dot(product_whole, gram, preferred_element_type=jnp.float32)]
    pallas_call x0 -> x3, Pallas kernels: none -> 61.3 us  [the longest x1 47.6 us: orthogonalize(): pl.pallas_call(orthogonalize_kernel, out_shape=jax.ShapeDtypeStruct((64,...]
    all_to_all x1, blocking collectives: 65.8 us -> 41.9 us  [body(): lax.all_to_all(blocks.reshape(128, 16, 512), ('shard', 'tensor'), split_a...]
  transfers between devices with their start and end apart: 9 -> 1, of which waited for: 9 -> 1; matrix products, arithmetic and copies ran while one was open for 0% -> 2% of each run, Pallas kernels for 0% -> 0%
where the time goes in v1:
time: 141 us; the launch traced here: 140 us
  Pallas kernels  61.3 us (43%)
  blocking collectives  41.9 us (30%)
  waiting for transfers between devices  27.2 us (19%)
  starting transfers between devices  3.87 us (3%)
  other arithmetic  3.19 us (2%)
  between operations  1.42 us (1%)
    pallas_call x1, Pallas kernels, orthogonalize(): pl.pallas_call(orthogonalize_kernel, out_shape=jax.ShapeDtypeStruct((64,...  47.6 us
    all_to_all x1, blocking collectives, body(): lax.all_to_all(blocks.reshape(128, 16, 512), ('shard', 'tensor'), split_a...  41.9 us
    all_to_all x1, waiting for transfers between devices, body(): lax.all_to_all(finished.reshape(128, 16, 512), ('shard', 'tensor'), split...  27.2 us
    pallas_call x1, Pallas kernels, advance(): pl.pallas_call(advance_kernel, grid=(64 // group,), in_specs=[pl.BlockSpe...  7.52 us
    pallas_call x1, Pallas kernels, place(): pl.pallas_call(place_kernel, grid=(64 // group,), in_specs=[pl.BlockSpec(...  6.21 us
    all_to_all x1, starting transfers between devices, body(): lax.all_to_all(finished.reshape(128, 16, 512), ('shard', 'tensor'), split...  3.87 us
    sub x2, other arithmetic, adamw(): weight - learn_rate * (first_new / (jnp.sqrt(second_new) + adam_floor) +...  3.19 us
  transfers between devices with their start and end apart: 1, of which 1 were waited for; matrix products, arithmetic and copies ran while one was open for 2% of the time, Pallas kernels for 0%

profile of v1, /device:TPU:1, one launch (start us, length us, event | category | flops | bytes accessed | tf_op | source)
XLA Modules:
  0.0 140.2 jit_solution(6313992062387581611)
XLA Ops:
  1.3 7.5 %shard_map.170 = (bf16[64,32,512]{2,1,0:T(8,128)(2,1)}, bf16[32,2,2,16,512]{4,3,2,1,0:T(8,128)(2,1)}) custom-call(s32[1]{0:T(128)S(6)} %copy.19.counts_ref, f32[64,32,512]{2,1,0:T(8,128)} %grads_ref.1, bf16[64,32,512]{2,1,0:T(8,128)(2,1)} %momentum_ref.1), custom_call_target="tpu_custom_call" | custom-call | tf_op jit(solution)/shard_map/pallas_call | solution.py:59
  8.8 41.9 %all_to_all.10 = bf16[128,16,512]{2,1,0:T(8,128)(2,1)S(1)} all-to-all(bf16[128,16,512]{2,1,0:T(8,128)(2,1)} %bitcast.7), channel_id=1, replica_groups=mesh['shard'=64,'tensor'=2] {'shard','tensor'}, dimensions={0} | all-to-all | bytes 4194304 | tf_op jit(solution)/shard_map/all_to_all | solution.py:262
  50.7 47.6 %shard_map.171 = bf16[64,2,16,512]{3,2,1,0:T(8,128)(2,1)} custom-call(bf16[64,2,16,512]{3,2,1,0:T(8,128)(2,1)S(1)} %bitcast.5), custom_call_target="tpu_custom_call" | custom-call | tf_op jit(solution)/shard_map/pallas_call | solution.py:223
  98.2 0.0 copy-start.3
  98.2 0.0 copy-start.4
  98.2 0.0 copy-start.5
  98.3 0.0 copy-start.6
  98.3 0.0 copy-start.1
  98.3 0.0 copy-start.2
  98.3 3.9 %all-to-all-start.1 = ((bf16[128,16,512]{2,1,0:T(8,128)(2,1)}), bf16[128,16,512]{2,1,0:T(8,128)(2,1)S(1)}, u32[]{:S(2)}, u32[]{:S(2)}) async-start(bf16[128,16,512]{2,1,0:T(8,128)(2,1)} %bitcast.2), calls=%async_computation.1 | async-start | bytes 4194304 | tf_op jit(solution)/shard_map/all_to_all | solution.py:266
  102.2 0.0 copy-done.3
  102.2 0.0 copy-done.4
  102.2 0.0 copy-done.5
  102.2 0.0 copy-done.6
  102.3 0.6 multiply_subtract_fusion.1
  102.9 0.0 copy-done.1
  102.9 0.0 copy-done.2
  102.9 2.6 %multiply_subtract_fusion = (f32[128,1024]{1,0:T(8,128)}, f32[128,1024]{1,0:T(8,128)}, f32[128,1024]{1,0:T(8,128)}) fusion(f32[128,1024]{1,0:T(8,128)S(1)} %copy-done.1, f32[128,1024]{1,0:T(8,128)S(1)} %copy-done.2, f32[]{:T(128)} %bitcast.4, f32[128,1024]{1,0:T(8,128)} %param.17, f32[128,1024]{1,0:T(8,128)} %param.16), kind=kLoop, calls=%fused_computation.2 | loop fusion | flops 1835008 | bytes 3670020 | tf_op jit(solution)/shard_map/sub | solution.py:36
  105.5 27.2 %all-to-all-done.1 = bf16[128,16,512]{2,1,0:T(8,128)(2,1)S(1)} async-done(((bf16[128,16,512]{2,1,0:T(8,128)(2,1)}), bf16[128,16,512]{2,1,0:T(8,128)(2,1)S(1)}, u32[]{:S(2)}, u32[]{:S(2)}) %all-to-all-start.1) | async-done | bytes 2097184 | tf_op jit(solution)/shard_map/all_to_all | solution.py:266
  132.7 0.0 copy-start
  132.7 1.3 copy-done
  134.0 6.2 %shard_map.172 = f32[64,32,512]{2,1,0:T(8,128)} custom-call(bf16[32,2,2,16,512]{4,3,2,1,0:T(8,128)(2,1)} %bitcast.6), custom_call_target="tpu_custom_call" | custom-call | tf_op jit(solution)/shard_map/pallas_call | solution.py:89
Async XLA Ops:
  98.2 4.0 %copy-start.3 = (f32[512]{0:T(512)S(1)}, f32[512]{0:T(512)}, u32[]{:S(2)}) copy-start(f32[512]{0:T(512)} %param.19) | copy-start | bytes 6148
  98.2 4.0 %copy-start.4 = (f32[512]{0:T(512)S(1)}, f32[512]{0:T(512)}, u32[]{:S(2)}) copy-start(f32[512]{0:T(512)} %param.18) | copy-start | bytes 6148
  98.2 4.0 %copy-start.5 = (f32[512]{0:T(512)S(1)}, f32[512]{0:T(512)}, u32[]{:S(2)}) copy-start(f32[512]{0:T(512)} %param.21) | copy-start | bytes 6148
  98.3 4.0 %copy-start.6 = (f32[512]{0:T(512)S(1)}, f32[512]{0:T(512)}, u32[]{:S(2)}) copy-start(f32[512]{0:T(512)} %param.20) | copy-start | bytes 6148
  98.3 4.6 %copy-start.1 = (f32[128,1024]{1,0:T(8,128)S(1)}, f32[128,1024]{1,0:T(8,128)}, u32[]{:S(2)}) copy-start(f32[128,1024]{1,0:T(8,128)} %param.15) | copy-start | bytes 1572868
  98.3 4.6 %copy-start.2 = (f32[128,1024]{1,0:T(8,128)S(1)}, f32[128,1024]{1,0:T(8,128)}, u32[]{:S(2)}) copy-start(f32[128,1024]{1,0:T(8,128)} %param.14) | copy-start | bytes 1572868
  98.3 34.4 %all-to-all-start.1 = ((bf16[128,16,512]{2,1,0:T(8,128)(2,1)}), bf16[128,16,512]{2,1,0:T(8,128)(2,1)S(1)}, u32[]{:S(2)}, u32[]{:S(2)}) async-start(bf16[128,16,512]{2,1,0:T(8,128)(2,1)} %bitcast.2), calls=%async_computation.1 | async-start | bytes 4194304 | tf_op jit(solution)/shard_map/all_to_all | solution.py:266
  132.7 1.3 copy-start
